TPU v7x, 512 devices: a whole 4x4x16 slice. The times are simulated.
512 devices in a mesh: dp: 4 (over y), expert: 128 (over x, z, core).
Axes of the slice: x: 4, y: 4, z: 16, core: 2. Of those that a mesh axis runs over, the one named last changes fastest.
Arguments:
- tokens: bfloat16 [1024, 4096], P('expert', 'dp'), may hold values from -6 to 6
- output_gradient: bfloat16 [1024, 4096], P('expert', 'dp'), may hold values from -6 to 6
- routes: int32 [1024, 8], P('expert'), may hold values from 0 to 63, all different within a row; in each aligned block of 8 rows (0 to 7, 8 to 15, ...) at most 2 rows name the same one
- router_expert_weight: bfloat16 [1024, 8], P('expert'), may hold values from 0.049804688 to 0.5
- tenant: int32 [1024], P('expert'), may hold values from 0 to 3
- gate_weight: bfloat16 [128, 4096, 512], P('expert', 'dp'), may hold values from -0.09375 to 0.09375
- up_weight: bfloat16 [128, 4096, 512], P('expert', 'dp'), may hold values from -0.09375 to 0.09375
- down_weight: bfloat16 [128, 512, 4096], P('expert', None, 'dp'), may hold values from -0.09375 to 0.09375
- adapter_input_maps: bfloat16 [128, 4096, 2, 4, 8], P('expert', 'dp'), may hold values from -0.09375 to 0.09375
- adapter_output_maps: bfloat16 [128, 2, 4, 16, 512], P('expert'), may hold values from -0.359375 to 0.359375
Outputs:
- input_grad: bfloat16 [1024, 4096], P('expert', 'dp')
- adapter_a_grad: float32 [128, 4096, 2, 4, 8], P('expert', 'dp')
- adapter_b_grad: float32 [128, 2, 4, 16, 512], P('expert')
Inputs may be any that keep to these rules, and one draw needn't show every extreme that they name: `routes`: among the 8 tokens of each aligned block of rows (the tokens of one index of the expert axis), no expert is chosen more than 2 times, a bound that some block reaches; a token's choices are distinct.
All inputs are finite; a program needn't handle non-finite values.
Results may differ from a plain program's by a relative error of at most 0.0065.
Values may be sent and summed in bfloat16 or wider, within the bound.
A program may use at most 64 MiB of HBM per device.

v0:
```python
import jax
import jax.numpy as jnp
from jax import lax
from jax.sharding import PartitionSpec as P

ADAPTER_SCALE = 2.0


def partner(shard, axis, bit):
    return lax.ppermute(shard, axis, [(i, i ^ 1 << bit) for i in range(lax.axis_size(axis))])


def product_leading(left, right):
    return lax.dot_general(
        left, right, (((0,), (0,)), ((), ())), preferred_element_type=jnp.float32
    )


def product_trailing(left, right):
    return lax.dot_general(
        left, right, (((1,), (1,)), ((), ())), preferred_element_type=jnp.float32
    )


def order_halves(mine, other, upper):
    return (jnp.where(upper, other, mine), jnp.where(upper, mine, other))


def spread(values, tenant_mask, tenant_list, adapter_rank_width):
    count = values.shape[0]
    wide = tenant_mask[:, None, :, None] * values.astype(jnp.float32).reshape(
        count, 2, 1, adapter_rank_width
    )
    return wide.reshape(count, 2, tenant_list * adapter_rank_width).astype(jnp.bfloat16)


def shards(
    tokens,
    output_gradient,
    routes,
    router_expert_weight,
    tenant,
    gate_weight,
    up_weight,
    down_weight,
    adapter_input_maps,
    adapter_output_maps,
):
    devices = lax.axis_size("expert")
    experts = devices // 2
    tok_col, quarter = tokens.shape
    topk = routes.shape[1]
    tenant_list = adapter_output_maps.shape[2]
    adapter_rank_width = adapter_output_maps.shape[3]
    hidden_halfway = adapter_output_maps.shape[4]
    rank_halfway = adapter_rank_width // 2
    capacity = 2 * tok_col * topk // experts
    half_cap = capacity // 2
    slots = devices * capacity
    upper = lax.axis_index("expert") % 2 == 1
    flat_route = routes.reshape(-1)
    expert_hot = (flat_route[:, None] == jnp.arange(experts, dtype=jnp.int32)[None, :]).astype(
        jnp.int32
    )
    earlier = jnp.cumsum(expert_hot, axis=0) - expert_hot
    position = jnp.sum(earlier * expert_hot, axis=1)
    slot_of = (flat_route * capacity + position).reshape(tok_col, topk)
    slot_range = jnp.arange(experts * capacity, dtype=jnp.int32)
    hits = (slot_range[:, None, None] == slot_of[None, :, :]).astype(jnp.float32)
    select_tok = jnp.sum(hits, axis=2)
    prob_tok = jnp.sum(hits * router_expert_weight.astype(jnp.float32)[None, :, :], axis=2)
    tenant_hot = (tenant[:, None] == jnp.arange(tenant_list, dtype=jnp.int32)[None, :]).astype(
        jnp.float32
    )
    select_bf = select_tok.astype(jnp.bfloat16)
    send_rows = jnp.dot(select_bf, tokens, preferred_element_type=jnp.float32).astype(jnp.bfloat16)
    send_grad = jnp.dot(select_bf, output_gradient, preferred_element_type=jnp.float32).astype(
        jnp.bfloat16
    )
    send_tag = jnp.dot(prob_tok, tenant_hot, precision=lax.Precision.HIGHEST).astype(jnp.bfloat16)

    def doubled(block):
        wide = block.reshape(experts, 1, capacity, block.shape[1])
        return jnp.broadcast_to(wide, (experts, 2, capacity, block.shape[1])).reshape(
            devices, capacity, block.shape[1]
        )

    got_rows, got_grad, got_tag = (
        lax.all_to_all(doubled(send_rows), "expert", split_axis=0, concat_axis=0, tiled=True),
        lax.all_to_all(doubled(send_grad), "expert", split_axis=0, concat_axis=0, tiled=True),
        lax.all_to_all(doubled(send_tag), "expert", split_axis=0, concat_axis=0, tiled=True),
    )
    input_rows = got_rows.reshape(slots, quarter)
    rows_dy = got_grad.reshape(slots, quarter)
    tags = got_tag.reshape(slots, tenant_list).astype(jnp.float32)
    tenant_mask = (tags > 0).astype(jnp.float32)
    slot_prob = jnp.sum(tags, axis=1)
    adapter_local = adapter_input_maps[0]
    adapter_other = partner(adapter_local, "expert", 0)
    low_rank, high_rank = order_halves(adapter_local, adapter_other, upper)
    adapter_cols = jnp.concatenate([low_rank, high_rank], axis=-1).reshape(
        quarter, 2 * tenant_list * adapter_rank_width
    )
    gate_output_map = adapter_output_maps[0, 0].reshape(
        tenant_list * adapter_rank_width, hidden_halfway
    )
    up_output_map = adapter_output_maps[0, 1].reshape(
        tenant_list * adapter_rank_width, hidden_halfway
    )
    gate_part = jnp.dot(input_rows, gate_weight[0], preferred_element_type=jnp.float32)
    up_part = jnp.dot(input_rows, up_weight[0], preferred_element_type=jnp.float32)
    act_part = product_trailing(rows_dy, down_weight[0])
    proj_all = jnp.dot(input_rows, adapter_cols, preferred_element_type=jnp.float32).reshape(
        slots, 2, tenant_list, adapter_rank_width
    )
    proj_part = jnp.sum(proj_all * tenant_mask[:, None, :, None], axis=2).reshape(
        slots, 2 * adapter_rank_width
    )
    gate_total, up_total, act_sum, proj_sum = lax.psum(
        (gate_part, up_part, act_part, proj_part), "dp"
    )
    proj_low = proj_sum.astype(jnp.bfloat16)
    spread_in = spread(proj_low, tenant_mask, tenant_list, adapter_rank_width)
    gate_preactivation = gate_total + ADAPTER_SCALE * jnp.dot(
        spread_in[:, 0], gate_output_map, preferred_element_type=jnp.float32
    )
    up_preactivation = up_total + ADAPTER_SCALE * jnp.dot(
        spread_in[:, 1], up_output_map, preferred_element_type=jnp.float32
    )
    act_grad = slot_prob[:, None] * act_sum
    gate_sig = jax.nn.sigmoid(gate_preactivation)
    gate_gradient = (
        act_grad * up_preactivation * gate_sig * (1.0 + gate_preactivation * (1.0 - gate_sig))
    ).astype(jnp.bfloat16)
    up_gradient = (act_grad * gate_preactivation * gate_sig).astype(jnp.bfloat16)
    gate_gradient, up_gradient, proj_low = (gate_gradient, up_gradient, proj_low)
    projection_spread = spread(proj_low, tenant_mask, tenant_list, adapter_rank_width)
    gate_output_map_gradient = ADAPTER_SCALE * product_leading(
        projection_spread[:, 0], gate_gradient
    )
    up_output_map_gradient = ADAPTER_SCALE * product_leading(projection_spread[:, 1], up_gradient)
    adapter_b_grad = jnp.stack([gate_output_map_gradient, up_output_map_gradient]).reshape(
        1, 2, tenant_list, adapter_rank_width, hidden_halfway
    )
    backward_total = ADAPTER_SCALE * jnp.stack(
        [
            product_trailing(gate_gradient, gate_output_map),
            product_trailing(up_gradient, up_output_map),
        ],
        axis=1,
    )
    back_part = jnp.sum(
        backward_total.reshape(slots, 2, tenant_list, adapter_rank_width)
        * tenant_mask[:, None, :, None],
        axis=2,
    ).reshape(slots, 2 * adapter_rank_width)
    input_part = product_trailing(gate_gradient, gate_weight[0]) + product_trailing(
        up_gradient, up_weight[0]
    )
    by_source = input_part.reshape(devices, capacity, quarter)
    first_half = by_source[:, :half_cap]
    second_half = by_source[:, half_cap:]
    keep_half = jnp.where(upper, second_half, first_half)
    give_half = jnp.where(upper, first_half, second_half)
    taken_half, back_other = partner((give_half, back_part), "expert", 0)
    input_half = keep_half + taken_half
    back_low = (back_part + back_other).astype(jnp.bfloat16)
    back_spread = spread(back_low, tenant_mask, tenant_list, adapter_rank_width)
    spread_rows = back_spread.reshape(devices, capacity, 2 * tenant_list * adapter_rank_width)
    spread_half = jnp.where(upper, spread_rows[:, half_cap:], spread_rows[:, :half_cap]).reshape(
        devices * half_cap, 2 * tenant_list * adapter_rank_width
    )
    adapter_term = product_trailing(spread_half, adapter_cols).reshape(devices, half_cap, quarter)
    slot_grad = (input_half + adapter_term).astype(jnp.bfloat16)
    spread_ranks = back_spread.reshape(slots, 2, tenant_list, adapter_rank_width)
    mine_cols = jnp.where(
        upper, spread_ranks[..., rank_halfway:], spread_ranks[..., :rank_halfway]
    ).reshape(slots, 2 * tenant_list * rank_halfway)
    adapter_a_grad = product_leading(input_rows, mine_cols).reshape(
        1, quarter, 2, tenant_list, rank_halfway
    )
    returned = lax.all_to_all(slot_grad, "expert", split_axis=0, concat_axis=0, tiled=True)
    slot_rows = returned.reshape(experts * capacity, quarter)
    input_grad = product_leading(select_bf, slot_rows).astype(jnp.bfloat16)
    return (input_grad, adapter_a_grad, adapter_b_grad)


def solution(mesh):
    placed = (
        P("expert", "dp"),
        P("expert", "dp"),
        P("expert", None),
        P("expert", None),
        P("expert"),
        P("expert", "dp", None),
        P("expert", "dp", None),
        P("expert", None, "dp"),
        P("expert", "dp", None, None, None),
        P("expert", None, None, None, None),
    )
    return jax.shard_map(
        shards,
        mesh=mesh,
        in_specs=placed,
        out_specs=(
            P("expert", "dp"),
            P("expert", "dp", None, None, None),
            P("expert", None, None, None, None),
        ),
        check_vma=False,
    )
```

profile of v0, /device:TPU:1, one launch (start us, length us, event | category | flops | bytes accessed | tf_op | source)
XLA Modules:
  0.0 237.5 jit_solution(15393630359983608216)
XLA Ops:
  10.2 1.1 broadcast_in_dim.17
  11.2 20.5 %all-to-all-start.2 = ((bf16[128,2,1024]{2,1,0:T(2,128)(2,1)}), bf16[128,2,1024]{2,1,0:T(2,128)(2,1)S(1)}, u32[]{:S(2)}, u32[]{:S(2)}) async-start(bf16[128,2,1024]{2,1,0:T(2,128)(2,1)} %bitcast.4), calls=%async_computation.2 | async-start | bytes 1048576 | tf_op jit(solution)/shard_map/all_to_all | solution.py:89
  32.2 32.8 %all-to-all-done.2 = bf16[128,2,1024]{2,1,0:T(2,128)(2,1)S(1)} async-done(((bf16[128,2,1024]{2,1,0:T(2,128)(2,1)}), bf16[128,2,1024]{2,1,0:T(2,128)(2,1)S(1)}, u32[]{:S(2)}, u32[]{:S(2)}) %all-to-all-start.2) | async-done | bytes 524320 | tf_op jit(solution)/shard_map/all_to_all | solution.py:89
  65.0 1.1 broadcast_in_dim.15
  66.0 7.7 %all-to-all-start.1 = ((bf16[128,2,1024]{2,1,0:T(2,128)(2,1)}), bf16[128,2,1024]{2,1,0:T(2,128)(2,1)}, u32[]{:S(2)}, u32[]{:S(2)}) async-start(bf16[128,2,1024]{2,1,0:T(2,128)(2,1)} %bitcast.2), calls=%async_computation.1 | async-start | bytes 1048576 | tf_op jit(solution)/shard_map/all_to_all | solution.py:90
  74.0 1.2 fusion.12
  75.3 1.2 fusion.9
  76.5 30.1 %all-to-all-done.1 = bf16[128,2,1024]{2,1,0:T(2,128)(2,1)} async-done(((bf16[128,2,1024]{2,1,0:T(2,128)(2,1)}), bf16[128,2,1024]{2,1,0:T(2,128)(2,1)}, u32[]{:S(2)}, u32[]{:S(2)}) %all-to-all-start.1) | async-done | bytes 524320 | tf_op jit(solution)/shard_map/all_to_all | solution.py:90
  106.6 1.2 reshape.132
  107.9 2.5 %fusion.14 = f32[256,512]{1,0:T(8,128)} fusion(bf16[256,1024]{1,0:T(8,128)(2,1)S(1)} %reshape.132, bf16[1,512,1024]{2,1,0:T(8,128)(2,1)} %param.17), kind=kOutput, calls=%fused_computation.28 | convolution fusion | flops 268435456 | bytes 2097152 | tf_op jit(solution)/shard_map/dot_general | solution.py:20
  111.3 3.2 %collective-permute-start = (bf16[1024,2,4,8]{0,3,2,1:T(8,128)(2,1)S(1)}, bf16[1024,2,4,8]{0,3,2,1:T(8,128)(2,1)}, u32[]{:S(2)}, u32[]{:S(2)}) collective-permute-start(bf16[1024,2,4,8]{0,3,2,1:T(8,128)(2,1)S(1)} %bitcast.122), channel_id=1, source_target_pairs={{0,1},{1,0},{2,3},{3,2},{4,5},{5,4},{6,7},{7,6},{8,9},{9,8},{10,11... | collective-permute-start | bytes 393224 | tf_op jit(solution)/shard_map/ppermute | solution.py:10
  115.6 6.1 %all-to-all-start = ((bf16[128,2,4]{2,1,0:T(2,128)(2,1)}), bf16[128,2,4]{2,1,0:T(2,128)(2,1)S(1)}, u32[]{:S(2)}, u32[]{:S(2)}) async-start(bf16[128,2,4]{2,1,0:T(2,128)(2,1)} %bitcast.1), calls=%async_computation | async-start | bytes 131072 | tf_op jit(solution)/shard_map/all_to_all | solution.py:91
  122.3 14.3 %all-to-all-done = bf16[128,2,4]{2,1,0:T(2,128)(2,1)S(1)} async-done(((bf16[128,2,4]{2,1,0:T(2,128)(2,1)}), bf16[128,2,4]{2,1,0:T(2,128)(2,1)S(1)}, u32[]{:S(2)}, u32[]{:S(2)}) %all-to-all-start) | async-done | bytes 2080 | tf_op jit(solution)/shard_map/all_to_all | solution.py:91
  137.7 0.9 broadcast_select_fusion.2
  139.4 1.0 reshape.148
  140.4 1.4 fusion.6
  141.8 13.6 %psum.30 = bf16[256,32]{0,1:T(8,128)(2,1)S(1)} all-reduce(f32[256,32]{0,1:T(8,128)S(1)} %bitcast.127), channel_id=1, replica_groups=mesh['dp'=4,'expert'=128] {'dp'}, use_global_device_ids=true, to_apply=%region_8.9 | all-reduce | flops 8192 | bytes 49152 | tf_op jit(solution)/shard_map/psum | solution.py:119
  155.4 13.2 %all-reduce.3.cloned.1.call-done = (f32[256,512]{1,0:T(8,128)}, f32[256,512]{1,0:T(8,128)}, f32[256,512]{1,0:T(8,128)}) async-done(((f32[256,512]{1,0:T(8,128)}, f32[256,512]{1,0:T(8,128)}, f32[256,512]{1,0:T(8,128)}), (f32[256,512]{1,0:T(8,128)}, f32[256,512]{1,0:T(8,128)}, f32[256,512]{1,0:T(8,128)})) %all-reduce.3.cloned.1.call-update) | async-done | bytes 1572880 | tf_op jit(solution)/shard_map/psum | solution.py:119
  168.6 1.6 multiply_convert_fusion
  172.2 2.8 %collective-permute-start.2 = (f32[256,32]{0,1:T(8,128)}, f32[256,32]{0,1:T(8,128)}, u32[]{:S(2)}, u32[]{:S(2)}) collective-permute-start(f32[256,32]{0,1:T(8,128)} %bitcast.28), channel_id=1, source_target_pairs={{0,1},{1,0},{2,3},{3,2},{4,5},{5,4},{6,7},{7,6},{8,9},{9,8},{10,11... | collective-permute-start | bytes 98312 | tf_op jit(solution)/shard_map/ppermute | solution.py:10
  174.9 1.5 convolution_add_fusion
  176.4 1.8 reshape.137
  179.0 1.0 copy_select_fusion
  180.0 1.9 collective-permute-start.1
  183.5 1.1 mul.175.clone
  184.7 1.4 mul.176
  186.1 1.0 multiply_convert_fusion.2
  187.2 1.3 add_convert_fusion
  189.9 0.9 reshape.152
  190.7 16.5 %all-to-all-start.3 = ((bf16[128,2,512]{2,1,0:T(2,128)(2,1)}), bf16[128,2,512]{2,1,0:T(2,128)(2,1)S(1)}, u32[]{:S(2)}, u32[]{:S(2)}) async-start(bf16[128,2,512]{2,1,0:T(2,128)(2,1)} %reshape.152), calls=%async_computation.3 | async-start | bytes 524288 | tf_op jit(solution)/shard_map/all_to_all | solution.py:182
  209.8 0.9 convolution_bitcast_fusion.1
  210.8 18.9 %all-to-all-done.3 = bf16[128,2,512]{2,1,0:T(2,128)(2,1)S(1)} async-done(((bf16[128,2,512]{2,1,0:T(2,128)(2,1)}), bf16[128,2,512]{2,1,0:T(2,128)(2,1)S(1)}, u32[]{:S(2)}, u32[]{:S(2)}) %all-to-all-start.3) | async-done | bytes 262176 | tf_op jit(solution)/shard_map/all_to_all | solution.py:182
  (96 shorter events, 17.2 us)
Async XLA Ops:
  7.2 68.1 %copy-start = (bf16[1,1024,512]{2,1,0:T(8,128)(2,1)S(1)}, bf16[1,1024,512]{2,1,0:T(8,128)(2,1)}, u32[]{:S(2)}) copy-start(bf16[1,1024,512]{2,1,0:T(8,128)(2,1)} %param.15) | copy-start | bytes 3145732
  8.4 0.7 copy-start.17
  8.4 0.7 copy-start.18
  9.1 0.7 copy-start.15
  9.2 22.6 %copy-start.13 = (bf16[128,8]{0,1:T(8,128)(2,1)}, bf16[128,8]{0,1:T(8,128)(2,1)S(1)}, u32[]{:S(2)}) copy-start(bf16[128,8]{0,1:T(8,128)(2,1)S(1)} %get-tuple-element.4) | copy-start | bytes 6148
  11.2 20.5 %copy-start.16 = (bf16[8,1024]{1,0:T(8,128)(2,1)S(1)}, bf16[8,1024]{1,0:T(8,128)(2,1)}, u32[]{:S(2)}) copy-start(bf16[8,1024]{1,0:T(8,128)(2,1)} %param.11) | copy-start | bytes 49156
  11.2 53.7 %all-to-all-start.2 = ((bf16[128,2,1024]{2,1,0:T(2,128)(2,1)}), bf16[128,2,1024]{2,1,0:T(2,128)(2,1)S(1)}, u32[]{:S(2)}, u32[]{:S(2)}) async-start(bf16[128,2,1024]{2,1,0:T(2,128)(2,1)} %bitcast.4), calls=%async_computation.2 | async-start | bytes 1048576 | tf_op jit(solution)/shard_map/all_to_all | solution.py:89
  66.0 8.0 %copy-start.1 = (bf16[1,1024,512]{2,1,0:T(8,128)(2,1)S(1)}, bf16[1,1024,512]{2,1,0:T(8,128)(2,1)}, u32[]{:S(2)}) copy-start(bf16[1,1024,512]{2,1,0:T(8,128)(2,1)} %param.16) | copy-start | bytes 3145732
  66.0 40.6 %all-to-all-start.1 = ((bf16[128,2,1024]{2,1,0:T(2,128)(2,1)}), bf16[128,2,1024]{2,1,0:T(2,128)(2,1)}, u32[]{:S(2)}, u32[]{:S(2)}) async-start(bf16[128,2,1024]{2,1,0:T(2,128)(2,1)} %bitcast.2), calls=%async_computation.1 | async-start | bytes 1048576 | tf_op jit(solution)/shard_map/all_to_all | solution.py:90
  73.8 94.8 %all-reduce.3.cloned.1.call-start = ((), (), s32[]{:S(2)}) async-start(), calls=%async_computation.4 | async-start | bytes 3145728 | tf_op jit(solution)/shard_map/psum | solution.py:119
  110.4 0.9 copy-start.9
  111.3 3.2 %copy-start.21 = (s32[8]{0:T(128)S(1)}, s32[8]{0:T(128)}, u32[]{:S(2)}) copy-start(s32[8]{0:T(128)} %param.14) | copy-start | bytes 100
  111.3 26.4 %collective-permute-start = (bf16[1024,2,4,8]{0,3,2,1:T(8,128)(2,1)S(1)}, bf16[1024,2,4,8]{0,3,2,1:T(8,128)(2,1)}, u32[]{:S(2)}, u32[]{:S(2)}) collective-permute-start(bf16[1024,2,4,8]{0,3,2,1:T(8,128)(2,1)S(1)} %bitcast.122), channel_id=1, source_target_pairs={{0,1},{1,0},{2,3},{3,2},{4,5},{5,4},{6,7},{7,6},{8,9},{9,8},{10,11... | collective-permute-start | bytes 393224 | tf_op jit(solution)/shard_map/ppermute | solution.py:10
  114.8 6.9 %copy-start.6 = (bf16[1,2,4,16,512]{4,3,2,1,0:T(8,128)(2,1)S(1)}, bf16[1,2,4,16,512]{4,3,2,1,0:T(8,128)(2,1)}, u32[]{:S(2)}) copy-start(bf16[1,2,4,16,512]{4,3,2,1,0:T(8,128)(2,1)} %param.19) | copy-start | bytes 393220
  115.6 21.1 %all-to-all-start = ((bf16[128,2,4]{2,1,0:T(2,128)(2,1)}), bf16[128,2,4]{2,1,0:T(2,128)(2,1)S(1)}, u32[]{:S(2)}, u32[]{:S(2)}) async-start(bf16[128,2,4]{2,1,0:T(2,128)(2,1)} %bitcast.1), calls=%async_computation | async-start | bytes 131072 | tf_op jit(solution)/shard_map/all_to_all | solution.py:91
  136.8 3.6 %copy-start.11 = (f32[256,4]{0,1:T(4,128)}, f32[256,4]{0,1:T(4,128)S(1)}, u32[]{:S(2)}) copy-start(f32[256,4]{0,1:T(4,128)S(1)} %copy.48) | copy-start | bytes 12292
  155.4 13.2 %copy-start.10 = (bf16[1,1,4,16,512]{4,3,2,1,0:T(8,128)(2,1)S(1)}, bf16[1,1,4,16,512]{4,3,2,1,0:T(8,128)(2,1)}, u32[]{:S(2)}) copy-start(bf16[1,1,4,16,512]{4,3,2,1,0:T(8,128)(2,1)} %get-tuple-element.12) | copy-start | bytes 196612
  155.4 14.8 %copy-start.7 = (bf16[256,2,64]{0,2,1:T(8,128)(2,1)}, bf16[256,2,64]{0,2,1:T(8,128)(2,1)S(1)}, u32[]{:S(2)}) copy-start(bf16[256,2,64]{0,2,1:T(8,128)(2,1)S(1)} %fusion.26) | copy-start | bytes 196612
  168.6 1.7 copy-start.19
  168.6 1.7 copy-start.20
  170.2 4.7 %copy-start.2 = (bf16[256,512]{1,0:T(8,128)(2,1)}, bf16[256,512]{1,0:T(8,128)(2,1)S(1)}, u32[]{:S(2)}) copy-start(bf16[256,512]{1,0:T(8,128)(2,1)S(1)} %get-tuple-element.16) | copy-start | bytes 786436
  172.2 9.8 %collective-permute-start.2 = (f32[256,32]{0,1:T(8,128)}, f32[256,32]{0,1:T(8,128)}, u32[]{:S(2)}, u32[]{:S(2)}) collective-permute-start(f32[256,32]{0,1:T(8,128)} %bitcast.28), channel_id=1, source_target_pairs={{0,1},{1,0},{2,3},{3,2},{4,5},{5,4},{6,7},{7,6},{8,9},{9,8},{10,11... | collective-permute-start | bytes 98312 | tf_op jit(solution)/shard_map/ppermute | solution.py:10
  180.0 7.2 %collective-permute-start.1 = (f32[128,1,1024]{2,0,1:T(8,128)}, f32[128,1,1024]{2,0,1:T(8,128)}, u32[]{:S(2)}, u32[]{:S(2)}) collective-permute-start(f32[128,1,1024]{2,0,1:T(8,128)} %copy_select_fusion), channel_id=1, source_target_pairs={{0,1},{1,0},{2,3},{3,2},{4,5},{5,4},{6,7},{7,6},{8,9},{9,8},{10,11... | collective-permute-start | bytes 1572872 | tf_op jit(solution)/shard_map/ppermute | solution.py:10
  186.1 1.2 copy-start.4
  190.7 16.5 %copy-start.8 = (bf16[256,2,64]{0,2,1:T(8,128)(2,1)S(1)}, bf16[256,2,64]{0,2,1:T(8,128)(2,1)}, u32[]{:S(2)}) copy-start(bf16[256,2,64]{0,2,1:T(8,128)(2,1)} %copy-done.7) | copy-start | bytes 196612
  190.7 38.9 %all-to-all-start.3 = ((bf16[128,2,512]{2,1,0:T(2,128)(2,1)}), bf16[128,2,512]{2,1,0:T(2,128)(2,1)S(1)}, u32[]{:S(2)}, u32[]{:S(2)}) async-start(bf16[128,2,512]{2,1,0:T(2,128)(2,1)} %reshape.152), calls=%async_computation.3 | async-start | bytes 524288 | tf_op jit(solution)/shard_map/all_to_all | solution.py:182
  207.3 1.0 copy-start.3
  208.2 1.6 copy-start.5
  209.1 0.7 copy-start.12
  210.7 19.1 %copy-start.14 = (bf16[128,8]{0,1:T(8,128)(2,1)S(1)}, bf16[128,8]{0,1:T(8,128)(2,1)}, u32[]{:S(2)}) copy-start(bf16[128,8]{0,1:T(8,128)(2,1)} %copy-done.13) | copy-start | bytes 6148
Sparse Core Ops, SparseCore 0:
  110.5 58.0 all-reduce.2
where the time goes:
time: 239 us; the launch traced here: 238 us
  waiting for transfers between devices  109 us (46%)
  starting transfers between devices  58.8 us (25%)
  local copies, waits for them, and re-layouts  19.2 us (8%)
  matrix products  14.8 us (6%)
  between operations  14.5 us (6%)
  blocking collectives  13.6 us (6%)
  other arithmetic  7.45 us (3%)
    all_to_all x1, waiting for transfers between devices, shards(): lax.all_to_all(doubled(send_rows), 'expert', split_axis=0, concat_axis=0,...  32.8 us
    all_to_all x1, waiting for transfers between devices, shards(): lax.all_to_all(doubled(send_grad), 'expert', split_axis=0, concat_axis=0,...  30.1 us
    all_to_all x1, starting transfers between devices, shards(): lax.all_to_all(doubled(send_rows), 'expert', split_axis=0, concat_axis=0,...  20.5 us
    all_to_all x1, waiting for transfers between devices, shards(): lax.all_to_all(slot_grad, 'expert', split_axis=0, concat_axis=0, tiled=True)  18.9 us
    all_to_all x1, starting transfers between devices, shards(): lax.all_to_all(slot_grad, 'expert', split_axis=0, concat_axis=0, tiled=True)  16.5 us
    all_to_all x1, waiting for transfers between devices, shards(): lax.all_to_all(doubled(send_tag), 'expert', split_axis=0, concat_axis=0,...  14.3 us
    psum x1, blocking collectives, shards(): lax.psum((gate_part, up_part, act_part, proj_part), 'dp')  13.6 us
    psum x1, waiting for transfers between devices, shards(): lax.psum((gate_part, up_part, act_part, proj_part), 'dp')  13.2 us
  transfers between devices with their start and end apart: 8, of which 5 were waited for; matrix products, arithmetic and copies ran while one was open for 9% of the time, Pallas kernels for 0%

commit v1 on v0

v1 whole, which is shorter than its diff:
```python
import functools

import jax
import jax.numpy as jnp
from jax import lax
from jax.experimental import pallas as pl
from jax.experimental.pallas import tpu as pltpu
from jax.sharding import PartitionSpec as P

ADAPTER_SCALE = 2.0
CHIPS_X = 4
BF = jnp.bfloat16
F32 = jnp.float32
MESH = pl.DeviceIdType.MESH


def mm(a, b):
    return lax.dot_general(a, b, (((1,), (0,)), ((), ())), preferred_element_type=F32)


def mm_t(a, b):
    return lax.dot_general(a, b, (((1,), (1,)), ((), ())), preferred_element_type=F32)


def iota(shape, axis):
    return lax.broadcasted_iota(jnp.int32, shape, axis)


def kernel(
    nx,
    nz,
    ny,
    tok,
    dy,
    routes,
    prob,
    ten,
    a_own,
    b_map,
    wg_hbm,
    wu_hbm,
    wd_hbm,
    ig_out,
    ag_out,
    bg_out,
    wg,
    wu,
    wd,
    pg,
    sel,
    rs,
    rr,
    afull,
    part_f,
    part_b,
    proj_f,
    proj_b,
    yr,
    yx,
    dgu,
    xsf,
    qs,
    qr,
    rsend,
    rrecv,
    sb,
    xb,
    tz,
    fb,
    w_sem,
    a_sem,
    ring_s,
    ring_r,
    xs_sem,
    xr_sem,
    cs_sem,
    cr_sem,
    ys_sem,
    yr_sem,
    gs_sem,
    gr_sem,
    q_sem,
    rc_s,
    rc_r,
    bx_s,
    bx_r,
    bz_s,
    bz_r,
):
    me = lax.axis_index("expert")
    y = lax.axis_index("dp")
    c = lax.rem(me, 2)
    z = lax.rem(lax.div(me, 2), nz)
    x = lax.div(me, 2 * nz)
    width = tok.shape[1]
    hid = wg.shape[1]
    ntok = tok.shape[0]
    lm = 2 * nx * nz
    pw = 2 * width + lm + 128
    sw = 2 * width + 128
    slots_x = 2 * nz
    half = pw // 2

    def eid(xx, zz, cc):
        return (xx * nz + zz) * 2 + cc

    partner = eid(x, z, 1 - c)
    zr = eid(x, lax.rem(z + 1, nz), c)
    zl = eid(x, lax.rem(z + nz - 1, nz), c)

    def rcopy(src, dst, s_sem, r_sem, dev):
        return pltpu.make_async_remote_copy(
            src_ref=src,
            dst_ref=dst,
            send_sem=s_sem,
            recv_sem=r_sem,
            device_id={"expert": dev},
            device_id_type=MESH,
        )

    def ycopy(src, dst, s_sem, r_sem, dev):
        return pltpu.make_async_remote_copy(
            src_ref=src,
            dst_ref=dst,
            send_sem=s_sem,
            recv_sem=r_sem,
            device_id={"dp": dev},
            device_id_type=MESH,
        )

    barrier = pltpu.get_barrier_semaphore()
    x_others = [lax.rem(x + d, nx) for d in ((2, 1, 3) if nx == 4 else range(1, nx))]
    y_others = [lax.rem(y + d, ny) for d in ((2, 1, 3) if ny == 4 else range(1, ny))]
    near = [zr, zl, partner] + [eid(o, z, c) for o in x_others]
    for dev in near:
        pl.semaphore_signal(barrier, inc=1, device_id={"expert": dev}, device_id_type=MESH)
    for dev in y_others:
        pl.semaphore_signal(barrier, inc=1, device_id={"dp": dev}, device_id_type=MESH)

    w_copies = [
        pltpu.make_async_copy(wg_hbm, wg, w_sem.at[0]),
        pltpu.make_async_copy(wu_hbm, wu, w_sem.at[1]),
        pltpu.make_async_copy(wd_hbm, wd, w_sem.at[2]),
    ]
    for w_copy in w_copies:
        w_copy.start()

    col = iota((ntok, lm), 1)
    row = iota((ntok, lm), 0)
    col_expert = lax.div(lax.rem(col, 2 * nx), 2) * nz + lax.div(col, 2 * nx)
    col_pos = lax.rem(col, 2)
    hit = jnp.zeros((ntok, lm), jnp.int32)
    weight = jnp.zeros((ntok, lm), F32)
    chosen = routes[...]
    probs = prob[...].astype(F32)
    for k in range(routes.shape[1]):
        same = chosen[:, k : k + 1] == col_expert
        hit = hit + same.astype(jnp.int32)
        weight = weight + jnp.where(same, probs[:, k : k + 1], 0.0)
    before = jnp.zeros((ntok, lm), jnp.int32)
    for n in range(ntok - 1):
        before = before + jnp.where(row > n, hit[n : n + 1, :], 0)
    weight = jnp.where(before == col_pos, weight, 0.0)
    lane_ten = lax.rem(lax.div(iota((ntok, 128), 1), 16), 4)
    ten_hot = (ten[...] == lane_ten).astype(F32)
    pg[z, :, 0:width] = tok[...]
    pg[z, :, width : 2 * width] = dy[...]
    pg[z, :, 2 * width : 2 * width + lm] = weight.astype(BF)
    pg[z, :, 2 * width + lm : pw] = ten_hot.astype(BF)
    afull[:, c] = a_own[...]

    pl.semaphore_wait(barrier, len(near) + len(y_others))

    a_copy = rcopy(a_own, afull.at[:, c], a_sem.at[0], a_sem.at[1], partner)

    far = nz // 2

    def ring(direction, step, piece):
        cols = pl.ds(piece * half, half)
        if direction == 0:
            block = lax.rem(z - step + 1 + nz, nz)
            dev = zr
        else:
            block = lax.rem(z + step - 1, nz)
            dev = zl
        ref = pg.at[block, :, cols]
        at = (direction * far + step - 1) * 2 + piece
        return rcopy(ref, ref, ring_s.at[at], ring_r.at[at], dev)

    sends = []
    for step in range(1, far + 1):
        for piece in range(2):
            for direction in range(2):
                if direction == 1 and step == far:
                    continue
                if step > 1:
                    ring(direction, step - 1, piece).wait_recv()
                copy = ring(direction, step, piece)
                copy.start()
                sends.append(copy)
        if step == 1:
            a_copy.start()
            sends.append(a_copy)
    for piece in range(2):
        ring(0, far, piece).wait_recv()
        if far > 1:
            ring(1, far - 1, piece).wait_recv()

    count = nz * ntok
    slots = nx * slots_x
    gathered = pg[...].astype(F32).reshape(count, pw).astype(BF)
    meta = gathered[:, 2 * width : 2 * width + lm]
    tenants = gathered[:, 2 * width + lm : pw]
    j = iota((slots, lm), 0)
    pick = (
        iota((slots, lm), 1) == z * (2 * nx) + lax.div(j, slots_x) * 2 + lax.rem(j, 2)
    ).astype(BF)
    slot_z = lax.div(lax.rem(iota((slots, count), 0), slots_x), 2)
    tok_z = lax.div(iota((slots, count), 1), ntok)
    weights_t = jnp.where(slot_z == tok_z, mm_t(pick, meta), 0.0)
    select_t = (weights_t > 0).astype(BF)
    slot_z2 = lax.div(lax.rem(iota((count, slots), 1), slots_x), 2)
    tok_z2 = lax.div(iota((count, slots), 0), ntok)
    weights_n = jnp.where(slot_z2 == tok_z2, mm_t(meta, pick), 0.0)
    sel[...] = (weights_n > 0).astype(BF)
    rs[:, :, 0 : 2 * width] = (
        mm(select_t, gathered[:, 0 : 2 * width]).astype(BF).reshape(nx, slots_x, 2 * width)
    )
    rs[:, :, 2 * width : sw] = (
        mm(weights_t.astype(BF), tenants).astype(BF).reshape(nx, slots_x, 128)
    )

    for i, o in enumerate(x_others):
        copy = rcopy(rs.at[o], rr.at[c, x], xs_sem.at[i], xr_sem.at[i], eid(o, z, c))
        copy.start()
        sends.append(copy)
    copy = rcopy(rs.at[x], rr.at[c, x], cs_sem.at[nx - 1], cr_sem.at[nx - 1], partner)
    copy.start()
    sends.append(copy)
    rr[c, x] = rs[x]
    back = (2, 3, 1) if nx == 4 else range(nx - 1, 0, -1)
    x_from = [lax.rem(x + d, nx) for d in back]
    for i, o in enumerate(x_from):
        block = rr.at[c, o]
        rcopy(block, block, xs_sem.at[i], xr_sem.at[i], eid(o, z, c)).wait_recv()
        copy = rcopy(block, block, cs_sem.at[i], cr_sem.at[i], partner)
        copy.start()
        sends.append(copy)
    for i, o in enumerate(x_from + [x]):
        block = rr.at[1 - c, o]
        rcopy(block, block, cs_sem.at[i], cr_sem.at[i], partner).wait_recv()
    rcopy(a_own, afull.at[:, 1 - c], a_sem.at[0], a_sem.at[1], partner).wait_recv()

    rows = 2 * slots
    quarter = rows // ny
    tag = rr[:, :, :, 2 * width : sw].reshape(rows, 128).astype(F32)
    mask = tag > 0
    slot_prob = jnp.max(tag, axis=1, keepdims=True)
    xin = rr[:, :, :, 0:width].reshape(rows, width)
    dyin = rr[:, :, :, width : 2 * width].reshape(rows, width)
    at = afull[...].astype(F32).reshape(128, width).astype(BF)

    def y_send(index, src, dst):
        for i, o in enumerate(y_others):
            copy = ycopy(src(o), dst, ys_sem.at[index, i], yr_sem.at[index, i], o)
            copy.start()
            sends.append(copy)

    def put(index, value):
        part_f[index] = value
        part_b[index] = value.astype(BF).reshape(ny, quarter, hid)
        y_send(index, lambda o: part_b.at[index, o], yr.at[index, y])

    w_copies[0].wait()
    put(0, mm(xin, wg[...]))
    w_copies[1].wait()
    put(1, mm(xin, wu[...]))
    w_copies[2].wait()
    put(2, mm_t(dyin, wd[...]) * slot_prob)
    projected = jnp.where(mask, mm_t(xin, at), 0.0)
    proj_f[...] = projected
    proj_b[...] = projected.astype(BF).reshape(ny, quarter, 128)
    y_send(3, lambda o: proj_b.at[o], yx.at[y])

    y_back = (2, 3, 1) if ny == 4 else range(ny - 1, 0, -1)
    y_from = [lax.rem(y + d, ny) for d in y_back]
    mine = pl.ds(pl.multiple_of(y * quarter, quarter), quarter)

    def total(index):
        value = part_f[index, mine, :]
        for i, o in enumerate(y_from):
            block = yr.at[index, o]
            ycopy(block, block, ys_sem.at[index, i], yr_sem.at[index, i], o).wait_recv()
            value = value + yr[index, o].astype(F32)
        return value

    gate = total(0)
    up = total(1)
    act = total(2)
    low = proj_f[mine, :]
    for i, o in enumerate(y_from):
        block = yx.at[o]
        ycopy(block, block, ys_sem.at[3, i], yr_sem.at[3, i], o).wait_recv()
        low = low + yx[o].astype(F32)
    lane = iota((quarter, 128), 1)
    bmap = b_map[...]
    gate = gate + ADAPTER_SCALE * mm(jnp.where(lane < 64, low, 0.0).astype(BF), bmap)
    up = up + ADAPTER_SCALE * mm(jnp.where(lane < 64, 0.0, low).astype(BF), bmap)
    sig = 1.0 / (1.0 + jnp.exp(-gate))
    dgu[y, :, 0:hid] = (act * up * sig * (1.0 + gate * (1.0 - sig))).astype(BF)
    dgu[y, :, hid : 2 * hid] = (act * gate * sig).astype(BF)
    xsf[y] = low.astype(BF)
    for i, o in enumerate(y_others):
        copy = ycopy(dgu.at[y], dgu.at[y], gs_sem.at[0, i], gr_sem.at[0, i], o)
        copy.start()
        sends.append(copy)
    for i, o in enumerate(y_others):
        copy = ycopy(xsf.at[y], xsf.at[y], gs_sem.at[1, i], gr_sem.at[1, i], o)
        copy.start()
        sends.append(copy)
    for i, o in enumerate(y_from):
        block = dgu.at[o]
        ycopy(block, block, gs_sem.at[0, i], gr_sem.at[0, i], o).wait_recv()
    for i, o in enumerate(y_from):
        block = xsf.at[o]
        ycopy(block, block, gs_sem.at[1, i], gr_sem.at[1, i], o).wait_recv()

    hq = ny // 2
    wide = iota((slots, 128), 1)

    def back_half(which):
        group = pl.ds(which * hq, hq)
        dg = dgu[group, :, 0:hid].reshape(slots, hid)
        du = dgu[group, :, hid : 2 * hid].reshape(slots, hid)
        marks = rr[which, :, :, 2 * width : sw].reshape(slots, 128).astype(F32) > 0
        q = jnp.where(wide < 64, mm_t(dg, bmap), mm_t(du, bmap))
        q = jnp.where(marks, ADAPTER_SCALE * q, 0.0)
        r = mm_t(dg, wg[...]) + mm_t(du, wu[...]) + mm(q.astype(BF), at)
        qs[which] = q
        return r.reshape(nx, slots_x, width)

    rsend[...] = back_half(1 - c).astype(BF)
    order = x_others + [x]
    order_from = x_from + [x]
    for i, o in enumerate(order):
        copy = rcopy(rsend.at[o], rrecv.at[o], rc_s.at[i], rc_r.at[i], partner)
        copy.start()
        sends.append(copy)
    sb[...] = back_half(c).astype(BF)
    q_copy = rcopy(qs, qr, q_sem.at[0], q_sem.at[1], partner)
    q_copy.start()
    sends.append(q_copy)
    for i, o in enumerate(order):
        block = rrecv.at[o]
        rcopy(block, block, rc_s.at[i], rc_r.at[i], partner).wait_recv()
        both = (sb[o].astype(F32) + rrecv[o].astype(F32)).astype(BF)
        if i < nx - 1:
            sb[o] = both
            copy = rcopy(sb.at[o], xb.at[x], bx_s.at[i], bx_r.at[i], eid(o, z, c))
            copy.start()
            sends.append(copy)
        else:
            xb[o] = both

    dg = dgu[:, :, 0:hid].reshape(rows, hid)
    du = dgu[:, :, hid : 2 * hid].reshape(rows, hid)
    low_t = xsf[...].reshape(rows, 128).astype(F32).T.astype(BF)
    bg_rows = iota((128, hid), 0)
    bg_out[...] = ADAPTER_SCALE * jnp.where(bg_rows < 64, mm(low_t, dg), mm(low_t, du))

    for i, o in enumerate(x_from):
        block = xb.at[o]
        rcopy(block, block, bx_s.at[i], bx_r.at[i], eid(o, z, c)).wait_recv()
    by_token = mm(sel[...], xb[...].reshape(slots, width))
    tz[...] = by_token.reshape(nz, ntok, width).astype(BF)
    dist = []
    for d in range(far, 0, -1):
        dist.append(d)
        if d != nz - d:
            dist.append(nz - d)
    for i, d in enumerate(dist):
        o = lax.rem(z + d, nz)
        copy = rcopy(tz.at[o], fb.at[z], bz_s.at[d - 1], bz_r.at[d - 1], eid(x, o, c))
        copy.start()
        sends.append(copy)
    fb[z] = tz[z]

    q_copy.wait_recv()
    q_all = (qs[...] + qr[...]).reshape(rows, 128)
    ag = mm(q_all.T.astype(BF), xin).reshape(8, 2, 8, width)
    ag_out[...] = jnp.where(c == 0, ag[:, 0], ag[:, 1])

    for d in dist:
        o = lax.rem(z + nz - d, nz)
        block = fb.at[o]
        rcopy(block, block, bz_s.at[d - 1], bz_r.at[d - 1], eid(x, o, c)).wait_recv()
    ig_out[...] = jnp.sum(fb[...].astype(F32), axis=0).astype(BF)
    for copy in sends:
        copy.wait_send()


def shards(
    tokens,
    output_gradient,
    routes,
    router_expert_weight,
    tenant,
    gate_weight,
    up_weight,
    down_weight,
    adapter_input_maps,
    adapter_output_maps,
    nx=CHIPS_X,
):
    devices = lax.axis_size("expert")
    ny = lax.axis_size("dp")
    nz = devices // (2 * nx)
    ntok, width = tokens.shape
    hid = gate_weight.shape[2]
    slots_x = 2 * nz
    slots = nx * slots_x
    rows = 2 * slots
    quarter = rows // ny
    lm = slots
    pw = 2 * width + lm + 128
    sw = 2 * width + 128
    a_own = jnp.transpose(adapter_input_maps[0], (1, 2, 3, 0)).reshape(8, 8, width)
    b_map = adapter_output_maps.reshape(128, hid)
    vmem = pl.BlockSpec(memory_space=pltpu.VMEM)
    anywhere = pl.BlockSpec(memory_space=pl.ANY)
    dma = pltpu.SemaphoreType.DMA
    far = nz // 2
    ig, ag, bg = pl.pallas_call(
        functools.partial(kernel, nx, nz, ny),
        out_shape=(
            jax.ShapeDtypeStruct((ntok, width), BF),
            jax.ShapeDtypeStruct((8, 8, width), F32),
            jax.ShapeDtypeStruct((128, hid), F32),
        ),
        in_specs=[vmem] * 7 + [anywhere] * 3,
        out_specs=(vmem, vmem, vmem),
        scratch_shapes=[
            pltpu.VMEM((width, hid), BF),
            pltpu.VMEM((width, hid), BF),
            pltpu.VMEM((hid, width), BF),
            pltpu.VMEM((nz, ntok, pw), BF),
            pltpu.VMEM((nz * ntok, slots), BF),
            pltpu.VMEM((nx, slots_x, sw), BF),
            pltpu.VMEM((2, nx, slots_x, sw), BF),
            pltpu.VMEM((8, 2, 8, width), BF),
            pltpu.VMEM((3, rows, hid), F32),
            pltpu.VMEM((3, ny, quarter, hid), BF),
            pltpu.VMEM((rows, 128), F32),
            pltpu.VMEM((ny, quarter, 128), BF),
            pltpu.VMEM((3, ny, quarter, hid), BF),
            pltpu.VMEM((ny, quarter, 128), BF),
            pltpu.VMEM((ny, quarter, 2 * hid), BF),
            pltpu.VMEM((ny, quarter, 128), BF),
            pltpu.VMEM((2, slots, 128), F32),
            pltpu.VMEM((2, slots, 128), F32),
            pltpu.VMEM((nx, slots_x, width), BF),
            pltpu.VMEM((nx, slots_x, width), BF),
            pltpu.VMEM((nx, slots_x, width), BF),
            pltpu.VMEM((nx, slots_x, width), BF),
            pltpu.VMEM((nz, ntok, width), BF),
            pltpu.VMEM((nz, ntok, width), BF),
            dma((3,)),
            dma((2,)),
            dma((4 * far,)),
            dma((4 * far,)),
            dma((nx - 1,)),
            dma((nx - 1,)),
            dma((nx,)),
            dma((nx,)),
            dma((4, ny - 1)),
            dma((4, ny - 1)),
            dma((2, ny - 1)),
            dma((2, ny - 1)),
            dma((2,)),
            dma((nx,)),
            dma((nx,)),
            dma((nx - 1,)),
            dma((nx - 1,)),
            dma((nz - 1,)),
            dma((nz - 1,)),
        ],
        compiler_params=pltpu.CompilerParams(collective_id=0, has_side_effects=True),
        name="layer_backward",
    )(
        tokens,
        output_gradient,
        routes,
        router_expert_weight,
        tenant.reshape(ntok, 1),
        a_own,
        b_map,
        gate_weight[0],
        up_weight[0],
        down_weight[0],
    )
    adapter_a_grad = jnp.transpose(ag.reshape(2, 4, 8, width), (3, 0, 1, 2))[None]
    adapter_b_grad = bg.reshape(1, 2, 4, 16, hid)
    return (ig, adapter_a_grad, adapter_b_grad)


def solution(mesh):
    placed = (
        P("expert", "dp"),
        P("expert", "dp"),
        P("expert", None),
        P("expert", None),
        P("expert"),
        P("expert", "dp", None),
        P("expert", "dp", None),
        P("expert", None, "dp"),
        P("expert", "dp", None, None, None),
        P("expert", None, None, None, None),
    )
    return jax.shard_map(
        shards,
        mesh=mesh,
        in_specs=placed,
        out_specs=(
            P("expert", "dp"),
            P("expert", "dp", None, None, None),
            P("expert", None, None, None, None),
        ),
        check_vma=False,
    )
```

time: 239 us -> 97.3 us (0.41)
  waiting for transfers between devices: 109 us -> 0 us
  Pallas kernels: 0 us -> 91.3 us
  starting transfers between devices: 58.8 us -> 0 us
  matrix products: 14.8 us -> 0 us
  local copies, waits for them, and re-layouts: 19.2 us -> 5.06 us
  between operations: 14.5 us -> 0.65 us
  blocking collectives: 13.6 us -> 0 us
  other arithmetic: 7.45 us -> 0 us
    all_to_all x4 -> x0, waiting for transfers between devices: 96.2 us -> none  [the longest x1 32.8 us: shards(): lax.all_to_all(doubled(send_rows), 'expert', split_axis=0, concat_axis=0,...]
    pallas_call x0 -> x1, Pallas kernels: none -> 91.3 us  [shards(): pl.pallas_call(functools.partial(kernel, nx, nz, ny), out_shape=(jax.Shap...]
    all_to_all x4 -> x0, starting transfers between devices: 50.8 us -> none  [the longest x1 20.5 us: shards(): lax.all_to_all(doubled(send_rows), 'expert', split_axis=0, concat_axis=0,...]
    dot_general x18 -> x0, matrix products: 14.8 us -> none  [the longest x6 6.13 us: product_trailing(): lax.dot_general(left, right, (((1,), (1,)), ((), ())), preferred_element_...]
    psum x1 -> x0, blocking collectives: 13.6 us -> none  [shards(): lax.psum((gate_part, up_part, act_part, proj_part), 'dp')]
    psum x1 -> x0, waiting for transfers between devices: 13.2 us -> none  [shards(): lax.psum((gate_part, up_part, act_part, proj_part), 'dp')]
    ppermute x3 -> x0, starting transfers between devices: 7.87 us -> none  [partner(): lax.ppermute(shard, axis, [(i, i ^ 1 << bit) for i in range(lax.axis_size...]
    reshape x4 -> x1, local copies, waits for them, and re-layouts: 4.31 us -> 0.67 us  [shards(): tenant.reshape(ntok, 1)]
  transfers between devices with their start and end apart: 8 -> 0, of which waited for: 5 -> 0; matrix products, arithmetic and copies ran while one was open for 9% -> 0% of each run, Pallas kernels for 0% -> 0%
where the time goes in v1:
time: 97.3 us; the launch traced here: 97 us
  Pallas kernels  91.3 us (94%)
  local copies, waits for them, and re-layouts  5.06 us (5%)
    pallas_call x1, Pallas kernels, shards(): pl.pallas_call(functools.partial(kernel, nx, nz, ny), out_shape=(jax.Shap...  91.3 us
    unnamed x7, local copies, waits for them, and re-layouts  4.39 us

profile of v1, /device:TPU:1, one launch (start us, length us, event | category | flops | bytes accessed | tf_op | source)
XLA Modules:
  0.0 97.0 jit_solution(5258007717941279661)
XLA Ops:
  0.6 0.0 copy-start.1
  0.6 0.6 copy-done.1
  1.3 0.7 copy.13.ten
  2.0 91.3 %layer_backward.1 = (bf16[8,1024]{1,0:T(8,128)(2,1)}, f32[8,8,1024]{2,1,0:T(8,128)}, f32[128,512]{1,0:T(8,128)}) custom-call(bf16[8,1024]{1,0:T(8,128)(2,1)} %tok.1, bf16[8,1024]{1,0:T(8,128)(2,1)} %dy.1, s32[8,8]{1,0:T(8,128)} %routes.1, bf16[8,8]{1,0:T(8,128)(2,1)} %prob.1, s32[8,1]{1,0:T(8,128)} %copy.13.ten, bf16[8,8,1024]{2,1,0:T(8,128)(2,1)} %bitcast.21, ...), custom_call_target="tpu_custom_call" | custom-call | tf_op jit(solution)/shard_map/layer_backward/pallas_call | solution.py:433
  93.3 1.3 %copy.17 = bf16[8,1024]{1,0:T(8,128)(2,1)} copy(bf16[8,1024]{1,0:T(8,128)(2,1)} %get-tuple-element.12) | data formatting | bytes 32768
  94.6 0.0 copy-start
  94.6 1.7 %copy.18 = f32[1,1024,2,4,8]{1,4,3,2,0:T(8,128)} copy(f32[1,1024,2,4,8]{1,4,3,2,0:T(8,128)} %bitcast.20) | data formatting | bytes 524288
  96.3 0.0 copy-done
  96.3 0.7 copy.19
Async XLA Ops:
  0.6 0.7 copy-start.1
  94.6 1.7 %copy-start = (f32[128,512]{1,0:T(8,128)S(1)}, f32[128,512]{1,0:T(8,128)}, u32[]{:S(2)}) copy-start(f32[128,512]{1,0:T(8,128)} %get-tuple-element.8) | copy-start | bytes 786436

commit v2 on v1

--- a/solution.py
+++ b/solution.py
@@ -9,6 +9,7 @@
 
 ADAPTER_SCALE = 2.0
 CHIPS_X = 4
+HOP = 2
 BF = jnp.bfloat16
 F32 = jnp.float32
 MESH = pl.DeviceIdType.MESH
@@ -99,14 +100,14 @@
     pw = 2 * width + lm + 128
     sw = 2 * width + 128
     slots_x = 2 * nz
-    half = pw // 2
 
     def eid(xx, zz, cc):
         return (xx * nz + zz) * 2 + cc
 
     partner = eid(x, z, 1 - c)
-    zr = eid(x, lax.rem(z + 1, nz), c)
-    zl = eid(x, lax.rem(z + nz - 1, nz), c)
+    z_near = []
+    for d in range(1, nz):
+        z_near.append(eid(x, lax.rem(z + d, nz), c))
 
     def rcopy(src, dst, s_sem, r_sem, dev):
         return pltpu.make_async_remote_copy(
@@ -131,7 +132,7 @@
     barrier = pltpu.get_barrier_semaphore()
     x_others = [lax.rem(x + d, nx) for d in ((2, 1, 3) if nx == 4 else range(1, nx))]
     y_others = [lax.rem(y + d, ny) for d in ((2, 1, 3) if ny == 4 else range(1, ny))]
-    near = [zr, zl, partner] + [eid(o, z, c) for o in x_others]
+    near = z_near + [partner] + [eid(o, z, c) for o in x_others]
     for dev in near:
         pl.semaphore_signal(barrier, inc=1, device_id={"expert": dev}, device_id_type=MESH)
     for dev in y_others:
@@ -175,36 +176,36 @@
 
     far = nz // 2
 
-    def ring(direction, step, piece):
-        cols = pl.ds(piece * half, half)
+    def ring(direction, d):
+        skip = min(d, HOP)
+        have = d - skip
         if direction == 0:
-            block = lax.rem(z - step + 1 + nz, nz)
-            dev = zr
+            block = lax.rem(z - have + nz, nz)
+            dev = lax.rem(z + skip, nz)
         else:
-            block = lax.rem(z + step - 1, nz)
-            dev = zl
-        ref = pg.at[block, :, cols]
-        at = (direction * far + step - 1) * 2 + piece
-        return rcopy(ref, ref, ring_s.at[at], ring_r.at[at], dev)
+            block = lax.rem(z + have, nz)
+            dev = lax.rem(z + nz - skip, nz)
+        ref = pg.at[block]
+        at = direction * far + d - 1
+        return rcopy(ref, ref, ring_s.at[at], ring_r.at[at], eid(x, dev, c))
 
     sends = []
-    for step in range(1, far + 1):
-        for piece in range(2):
-            for direction in range(2):
-                if direction == 1 and step == far:
-                    continue
-                if step > 1:
-                    ring(direction, step - 1, piece).wait_recv()
-                copy = ring(direction, step, piece)
-                copy.start()
-                sends.append(copy)
-        if step == 1:
+    for d in range(1, far + 1):
+        for direction in range(2):
+            if direction == 1 and d == far:
+                continue
+            if d > HOP:
+                ring(direction, d - HOP).wait_recv()
+            copy = ring(direction, d)
+            copy.start()
+            sends.append(copy)
+        if d == min(HOP, far):
             a_copy.start()
             sends.append(a_copy)
-    for piece in range(2):
-        ring(0, far, piece).wait_recv()
-        if far > 1:
-            ring(1, far - 1, piece).wait_recv()
+    for direction in range(2):
+        last = far - direction
+        for d in range(max(1, last - HOP + 1), last + 1):
+            ring(direction, d).wait_recv()
 
     count = nz * ntok
     slots = nx * slots_x
@@ -466,8 +467,8 @@
             pltpu.VMEM((nz, ntok, width), BF),
             dma((3,)),
             dma((2,)),
-            dma((4 * far,)),
-            dma((4 * far,)),
+            dma((2 * far,)),
+            dma((2 * far,)),
             dma((nx - 1,)),
             dma((nx - 1,)),
             dma((nx,)),

time: 97.3 us -> 91.5 us (0.940)
  Pallas kernels: 91.3 us -> 85.5 us
    pallas_call x1, Pallas kernels: 91.3 us -> 85.5 us  [shards(): pl.pallas_call(functools.partial(kernel, nx, nz, ny), out_shape=(jax.Shap...]
where the time goes in v2:
time: 91.5 us; the launch traced here: 91.3 us
  Pallas kernels  85.5 us (93%)
  local copies, waits for them, and re-layouts  5.06 us (6%)
    pallas_call x1, Pallas kernels, shards(): pl.pallas_call(functools.partial(kernel, nx, nz, ny), out_shape=(jax.Shap...  85.5 us
    unnamed x7, local copies, waits for them, and re-layouts  4.39 us

profile of v2, /device:TPU:1, one launch (start us, length us, event | category | flops | bytes accessed | tf_op | source)
XLA Modules:
  0.0 91.3 jit_solution(10587376028678712729)
XLA Ops:
  0.6 0.0 copy-start.1
  0.6 0.6 copy-done.1
  1.3 0.7 copy.13.ten
  2.0 85.5 %layer_backward.1 = (bf16[8,1024]{1,0:T(8,128)(2,1)}, f32[8,8,1024]{2,1,0:T(8,128)}, f32[128,512]{1,0:T(8,128)}) custom-call(bf16[8,1024]{1,0:T(8,128)(2,1)} %tok.1, bf16[8,1024]{1,0:T(8,128)(2,1)} %dy.1, s32[8,8]{1,0:T(8,128)} %routes.1, bf16[8,8]{1,0:T(8,128)(2,1)} %prob.1, s32[8,1]{1,0:T(8,128)} %copy.13.ten, bf16[8,8,1024]{2,1,0:T(8,128)(2,1)} %bitcast.21, ...), custom_call_target="tpu_custom_call" | custom-call | tf_op jit(solution)/shard_map/layer_backward/pallas_call | solution.py:434
  87.5 1.3 %copy.17 = bf16[8,1024]{1,0:T(8,128)(2,1)} copy(bf16[8,1024]{1,0:T(8,128)(2,1)} %get-tuple-element.12) | data formatting | bytes 32768
  88.8 0.0 copy-start
  88.8 1.7 %copy.18 = f32[1,1024,2,4,8]{1,4,3,2,0:T(8,128)} copy(f32[1,1024,2,4,8]{1,4,3,2,0:T(8,128)} %bitcast.20) | data formatting | bytes 524288
  90.6 0.0 copy-done
  90.6 0.7 copy.19
Async XLA Ops:
  0.6 0.7 copy-start.1
  88.8 1.7 %copy-start = (f32[128,512]{1,0:T(8,128)S(1)}, f32[128,512]{1,0:T(8,128)}, u32[]{:S(2)}) copy-start(f32[128,512]{1,0:T(8,128)} %get-tuple-element.8) | copy-start | bytes 786436

commit v3 on v2

v3 whole, which is shorter than its diff:
```python
import functools

import jax
import jax.numpy as jnp
from jax import lax
from jax.experimental import pallas as pl
from jax.experimental.pallas import tpu as pltpu
from jax.sharding import PartitionSpec as P

ADAPTER_SCALE = 2.0
CHIPS_X = 4
HOP = 2
GROUPS = 2
BF = jnp.bfloat16
F32 = jnp.float32
MESH = pl.DeviceIdType.MESH


def mm(a, b):
    return lax.dot_general(a, b, (((1,), (0,)), ((), ())), preferred_element_type=F32)


def mm_t(a, b):
    return lax.dot_general(a, b, (((1,), (1,)), ((), ())), preferred_element_type=F32)


def iota(shape, axis):
    return lax.broadcasted_iota(jnp.int32, shape, axis)


def kernel(
    nx,
    nz,
    ny,
    tok,
    dy,
    routes,
    prob,
    ten,
    a_own,
    b_map,
    wg_hbm,
    wu_hbm,
    wd_hbm,
    ig_out,
    ag_out,
    bg_out,
    wg,
    wu,
    wd,
    pg,
    sel,
    rs,
    rr,
    afull,
    part_f,
    part_b,
    proj_f,
    proj_b,
    yr,
    yx,
    dgu,
    xsf,
    qs,
    qr,
    rfull,
    rrecv,
    sb,
    xb,
    tz,
    fb,
    w_sem,
    a_sem,
    ring_s,
    ring_r,
    xs_sem,
    xr_sem,
    cs_sem,
    cr_sem,
    ys_sem,
    yr_sem,
    gs_sem,
    gr_sem,
    q_sem,
    rc_s,
    rc_r,
    bx_s,
    bx_r,
    bz_s,
    bz_r,
):
    me = lax.axis_index("expert")
    y = lax.axis_index("dp")
    c = lax.rem(me, 2)
    z = lax.rem(lax.div(me, 2), nz)
    x = lax.div(me, 2 * nz)
    width = tok.shape[1]
    hid = wg.shape[1]
    ntok = tok.shape[0]
    lm = 2 * nx * nz
    pw = 2 * width + lm + 128
    sw = 2 * width + 128
    far = nz // 2
    gz = nz // GROUPS
    off = gz // 2 - 1
    slots_x = 2 * gz
    slots = nx * slots_x
    rows = 2 * slots
    quarter = rows // ny
    count = gz * ntok

    def eid(xx, zz, cc):
        return (xx * nz + zz) * 2 + cc

    partner = eid(x, z, 1 - c)
    z_near = []
    for d in range(1, nz):
        z_near.append(eid(x, lax.rem(z + d, nz), c))

    def rcopy(src, dst, s_sem, r_sem, dev):
        return pltpu.make_async_remote_copy(
            src_ref=src,
            dst_ref=dst,
            send_sem=s_sem,
            recv_sem=r_sem,
            device_id={"expert": dev},
            device_id_type=MESH,
        )

    def ycopy(src, dst, s_sem, r_sem, dev):
        return pltpu.make_async_remote_copy(
            src_ref=src,
            dst_ref=dst,
            send_sem=s_sem,
            recv_sem=r_sem,
            device_id={"dp": dev},
            device_id_type=MESH,
        )

    barrier = pltpu.get_barrier_semaphore()
    x_others = [lax.rem(x + d, nx) for d in ((2, 1, 3) if nx == 4 else range(1, nx))]
    y_others = [lax.rem(y + d, ny) for d in ((2, 1, 3) if ny == 4 else range(1, ny))]
    near = z_near + [partner] + [eid(o, z, c) for o in x_others]
    for dev in near:
        pl.semaphore_signal(barrier, inc=1, device_id={"expert": dev}, device_id_type=MESH)
    for dev in y_others:
        pl.semaphore_signal(barrier, inc=1, device_id={"dp": dev}, device_id_type=MESH)

    w_copies = [
        pltpu.make_async_copy(wg_hbm, wg, w_sem.at[0]),
        pltpu.make_async_copy(wu_hbm, wu, w_sem.at[1]),
        pltpu.make_async_copy(wd_hbm, wd, w_sem.at[2]),
    ]
    for w_copy in w_copies:
        w_copy.start()

    col = iota((ntok, lm), 1)
    row = iota((ntok, lm), 0)
    col_expert = lax.div(lax.rem(col, 2 * nx), 2) * nz + lax.div(col, 2 * nx)
    col_pos = lax.rem(col, 2)
    hit = jnp.zeros((ntok, lm), jnp.int32)
    weight = jnp.zeros((ntok, lm), F32)
    chosen = routes[...]
    probs = prob[...].astype(F32)
    for k in range(routes.shape[1]):
        same = chosen[:, k : k + 1] == col_expert
        hit = hit + same.astype(jnp.int32)
        weight = weight + jnp.where(same, probs[:, k : k + 1], 0.0)
    before = jnp.zeros((ntok, lm), jnp.int32)
    for n in range(ntok - 1):
        before = before + jnp.where(row > n, hit[n : n + 1, :], 0)
    weight = jnp.where(before == col_pos, weight, 0.0)
    lane_ten = lax.rem(lax.div(iota((ntok, 128), 1), 16), 4)
    ten_hot = (ten[...] == lane_ten).astype(F32)
    pg[off, :, 0:width] = tok[...]
    pg[off, :, width : 2 * width] = dy[...]
    pg[off, :, 2 * width : 2 * width + lm] = weight.astype(BF)
    pg[off, :, 2 * width + lm : pw] = ten_hot.astype(BF)
    afull[:, c] = a_own[...]

    pl.semaphore_wait(barrier, len(near) + len(y_others))

    a_copy = rcopy(a_own, afull.at[:, c], a_sem.at[0], a_sem.at[1], partner)

    sends = []
    arrived = set()

    def place(direction, d):
        return (off - d) % nz if direction == 0 else (off + d) % nz

    def ring(direction, d):
        skip = min(d, HOP)
        dev = lax.rem(z + skip, nz) if direction == 0 else lax.rem(z + nz - skip, nz)
        at = direction * far + d - 1
        return rcopy(
            pg.at[place(direction, d - skip)],
            pg.at[place(direction, d)],
            ring_s.at[at],
            ring_r.at[at],
            eid(x, dev, c),
        )

    def need(direction, d):
        if d > 0 and (direction, d) not in arrived:
            arrived.add((direction, d))
            ring(direction, d).wait_recv()

    def send(copy):
        copy.start()
        sends.append(copy)

    def advance(first, last):
        for d in range(first, last + 1):
            for direction in range(2):
                if direction == 1 and d == far:
                    continue
                need(direction, d - HOP)
                send(ring(direction, d))

    def select(g):
        gathered = pg[g * gz : (g + 1) * gz].astype(F32).reshape(count, pw).astype(BF)
        meta = gathered[:, 2 * width : 2 * width + lm]
        tenants = gathered[:, 2 * width + lm : pw]
        j = iota((slots, lm), 0)
        pick = (
            iota((slots, lm), 1) == z * (2 * nx) + lax.div(j, slots_x) * 2 + lax.rem(j, 2)
        ).astype(BF)
        slot_z = lax.div(lax.rem(iota((slots, count), 0), slots_x), 2)
        tok_z = lax.div(iota((slots, count), 1), ntok)
        weights_t = jnp.where(slot_z == tok_z, mm_t(pick, meta), 0.0)
        select_t = (weights_t > 0).astype(BF)
        slot_z2 = lax.div(lax.rem(iota((count, slots), 1), slots_x), 2)
        tok_z2 = lax.div(iota((count, slots), 0), ntok)
        weights_n = jnp.where(slot_z2 == tok_z2, mm_t(meta, pick), 0.0)
        sel[g] = (weights_n > 0).astype(BF)
        rs[g, :, :, 0 : 2 * width] = (
            mm(select_t, gathered[:, 0 : 2 * width]).astype(BF).reshape(nx, slots_x, 2 * width)
        )
        rs[g, :, :, 2 * width : sw] = (
            mm(weights_t.astype(BF), tenants).astype(BF).reshape(nx, slots_x, 128)
        )

    back = (2, 3, 1) if nx == 4 else range(nx - 1, 0, -1)
    x_from = [lax.rem(x + d, nx) for d in back]

    def x_send(g):
        for i, o in enumerate(x_others):
            send(rcopy(rs.at[g, o], rr.at[g, c, x], xs_sem.at[g, i], xr_sem.at[g, i], eid(o, z, c)))
        last = nx - 1
        send(rcopy(rs.at[g, x], rr.at[g, c, x], cs_sem.at[g, last], cr_sem.at[g, last], partner))
        rr[g, c, x] = rs[g, x]

    def x_recv(g):
        for i, o in enumerate(x_from):
            block = rr.at[g, c, o]
            rcopy(block, block, xs_sem.at[g, i], xr_sem.at[g, i], eid(o, z, c)).wait_recv()
            send(rcopy(block, block, cs_sem.at[g, i], cr_sem.at[g, i], partner))

    def c_recv(g):
        for i, o in enumerate(x_from + [x]):
            block = rr.at[g, 1 - c, o]
            rcopy(block, block, cs_sem.at[g, i], cr_sem.at[g, i], partner).wait_recv()

    bmap = b_map[...]

    def adapters():
        return afull[...].astype(F32).reshape(128, width).astype(BF)

    def marks(g):
        return rr[g, :, :, :, 2 * width : sw].reshape(rows, 128).astype(F32)

    def y_send(g, index, src, dst):
        for i, o in enumerate(y_others):
            send(ycopy(src(o), dst, ys_sem.at[g, index, i], yr_sem.at[g, index, i], o))

    def partial(g):
        tag = marks(g)
        slot_prob = jnp.max(tag, axis=1, keepdims=True)
        xin = rr[g, :, :, :, 0:width].reshape(rows, width)
        dyin = rr[g, :, :, :, width : 2 * width].reshape(rows, width)

        def put(index, value):
            part_f[g, index] = value
            part_b[g, index] = value.astype(BF).reshape(ny, quarter, hid)
            y_send(g, index, lambda o: part_b.at[g, index, o], yr.at[g, index, y])

        if g == 0:
            w_copies[0].wait()
        put(0, mm(xin, wg[...]))
        if g == 0:
            w_copies[1].wait()
        put(1, mm(xin, wu[...]))
        if g == 0:
            w_copies[2].wait()
        put(2, mm_t(dyin, wd[...]) * slot_prob)
        projected = jnp.where(tag > 0, mm_t(xin, adapters()), 0.0)
        proj_f[g] = projected
        proj_b[g] = projected.astype(BF).reshape(ny, quarter, 128)
        y_send(g, 3, lambda o: proj_b.at[g, o], yx.at[g, y])

    y_back = (2, 3, 1) if ny == 4 else range(ny - 1, 0, -1)
    y_from = [lax.rem(y + d, ny) for d in y_back]
    mine = pl.ds(pl.multiple_of(y * quarter, quarter), quarter)

    def total(g, index):
        value = part_f[g, index, mine, :]
        for i, o in enumerate(y_from):
            block = yr.at[g, index, o]
            ycopy(block, block, ys_sem.at[g, index, i], yr_sem.at[g, index, i], o).wait_recv()
            value = value + yr[g, index, o].astype(F32)
        return value

    def act_grads(g):
        gate = total(g, 0)
        up = total(g, 1)
        act = total(g, 2)
        low = proj_f[g, mine, :]
        for i, o in enumerate(y_from):
            block = yx.at[g, o]
            ycopy(block, block, ys_sem.at[g, 3, i], yr_sem.at[g, 3, i], o).wait_recv()
            low = low + yx[g, o].astype(F32)
        lane = iota((quarter, 128), 1)
        gate = gate + ADAPTER_SCALE * mm(jnp.where(lane < 64, low, 0.0).astype(BF), bmap)
        up = up + ADAPTER_SCALE * mm(jnp.where(lane < 64, 0.0, low).astype(BF), bmap)
        sig = 1.0 / (1.0 + jnp.exp(-gate))
        dgu[g, y, :, 0:hid] = (act * up * sig * (1.0 + gate * (1.0 - sig))).astype(BF)
        dgu[g, y, :, hid : 2 * hid] = (act * gate * sig).astype(BF)
        xsf[g, y] = low.astype(BF)
        for k, ref in enumerate((dgu, xsf)):
            mine_of = ref.at[g, y]
            for i, o in enumerate(y_others):
                send(ycopy(mine_of, mine_of, gs_sem.at[g, k, i], gr_sem.at[g, k, i], o))

    def g_recv(g):
        for k, ref in enumerate((dgu, xsf)):
            for i, o in enumerate(y_from):
                block = ref.at[g, o]
                ycopy(block, block, gs_sem.at[g, k, i], gr_sem.at[g, k, i], o).wait_recv()

    order = x_others + [x]

    def back_send(g):
        dg = dgu[g, :, :, 0:hid].reshape(rows, hid)
        du = dgu[g, :, :, hid : 2 * hid].reshape(rows, hid)
        wide = iota((rows, 128), 1)
        q = jnp.where(wide < 64, mm_t(dg, bmap), mm_t(du, bmap))
        q = jnp.where(marks(g) > 0, ADAPTER_SCALE * q, 0.0)
        r = mm_t(dg, wg[...]) + mm_t(du, wu[...]) + mm(q.astype(BF), adapters())
        qs[g] = q
        rfull[g] = r.astype(BF).reshape(2, nx, slots_x, width)
        for i, o in enumerate(order):
            send(rcopy(rfull.at[g, 1 - c, o], rrecv.at[g, o], rc_s.at[g, i], rc_r.at[g, i], partner))
        send(q_copy(g))

    def q_copy(g):
        return rcopy(qs.at[g], qr.at[g], q_sem.at[g, 0], q_sem.at[g, 1], partner)

    def back_x(g):
        for i, o in enumerate(order):
            block = rrecv.at[g, o]
            rcopy(block, block, rc_s.at[g, i], rc_r.at[g, i], partner).wait_recv()
            both = (rfull[g, c, o].astype(F32) + rrecv[g, o].astype(F32)).astype(BF)
            if i < nx - 1:
                sb[g, o] = both
                send(rcopy(sb.at[g, o], xb.at[g, x], bx_s.at[g, i], bx_r.at[g, i], eid(o, z, c)))
            else:
                xb[g, o] = both

    def home(g):
        for i, o in enumerate(x_from):
            block = xb.at[g, o]
            rcopy(block, block, bx_s.at[g, i], bx_r.at[g, i], eid(o, z, c)).wait_recv()
        by_token = mm(sel[g], xb[g].reshape(slots, width))
        tz[g * gz : (g + 1) * gz] = by_token.reshape(gz, ntok, width).astype(BF)
        dist = [(q - off) % nz for q in range(g * gz, (g + 1) * gz)]
        for d in sorted(dist, key=lambda d: -min(d, nz - d)):
            q = (d + off) % nz
            if d == 0:
                fb[0] = tz[q]
                continue
            o = lax.rem(z + d, nz)
            send(rcopy(tz.at[q], fb.at[d], bz_s.at[d - 1], bz_r.at[d - 1], eid(x, o, c)))

    step = min(HOP, far)
    advance(1, step)
    send(a_copy)
    advance(step + 1, max(step, far - HOP))
    for d in range(1, off + 1):
        need(0, d)
    for d in range(1, gz - off):
        need(1, d)
    select(0)
    x_send(0)
    advance(max(step, far - HOP) + 1, far)
    x_recv(0)
    for d in range(1, far + 1):
        need(0, d)
        if d < far:
            need(1, d)
    select(1)
    x_send(1)
    rcopy(a_own, afull.at[:, 1 - c], a_sem.at[0], a_sem.at[1], partner).wait_recv()
    c_recv(0)
    partial(0)
    x_recv(1)
    act_grads(0)
    c_recv(1)
    partial(1)
    g_recv(0)
    back_send(0)
    act_grads(1)
    back_x(0)
    home(0)
    g_recv(1)
    back_send(1)
    back_x(1)

    every = GROUPS * rows
    dg = dgu[:, :, :, 0:hid].reshape(every, hid)
    du = dgu[:, :, :, hid : 2 * hid].reshape(every, hid)
    low_t = xsf[...].reshape(every, 128).astype(F32).T.astype(BF)
    bg_rows = iota((128, hid), 0)
    bg_out[...] = ADAPTER_SCALE * jnp.where(bg_rows < 64, mm(low_t, dg), mm(low_t, du))
    home(1)

    for g in range(GROUPS):
        q_copy(g).wait_recv()
    q_all = (qs[...] + qr[...]).reshape(every, 128)
    xin = rr[:, :, :, :, 0:width].reshape(every, width)
    ag = mm(q_all.T.astype(BF), xin).reshape(8, 2, 8, width)
    ag_out[...] = jnp.where(c == 0, ag[:, 0], ag[:, 1])

    for d in range(1, nz):
        o = lax.rem(z + nz - d, nz)
        block = fb.at[d]
        rcopy(block, block, bz_s.at[d - 1], bz_r.at[d - 1], eid(x, o, c)).wait_recv()
    ig_out[...] = jnp.sum(fb[...].astype(F32), axis=0).astype(BF)
    for copy in sends:
        copy.wait_send()


def shards(
    tokens,
    output_gradient,
    routes,
    router_expert_weight,
    tenant,
    gate_weight,
    up_weight,
    down_weight,
    adapter_input_maps,
    adapter_output_maps,
    nx=CHIPS_X,
):
    devices = lax.axis_size("expert")
    ny = lax.axis_size("dp")
    nz = devices // (2 * nx)
    ntok, width = tokens.shape
    hid = gate_weight.shape[2]
    slots_x = 2 * nz // GROUPS
    slots = nx * slots_x
    rows = 2 * slots
    quarter = rows // ny
    count = nz // GROUPS * ntok
    lm = 2 * nx * nz
    pw = 2 * width + lm + 128
    sw = 2 * width + 128
    a_own = jnp.transpose(adapter_input_maps[0], (1, 2, 3, 0)).reshape(8, 8, width)
    b_map = adapter_output_maps.reshape(128, hid)
    vmem = pl.BlockSpec(memory_space=pltpu.VMEM)
    anywhere = pl.BlockSpec(memory_space=pl.ANY)
    dma = pltpu.SemaphoreType.DMA
    far = nz // 2
    ig, ag, bg = pl.pallas_call(
        functools.partial(kernel, nx, nz, ny),
        out_shape=(
            jax.ShapeDtypeStruct((ntok, width), BF),
            jax.ShapeDtypeStruct((8, 8, width), F32),
            jax.ShapeDtypeStruct((128, hid), F32),
        ),
        in_specs=[vmem] * 7 + [anywhere] * 3,
        out_specs=(vmem, vmem, vmem),
        scratch_shapes=[
            pltpu.VMEM((width, hid), BF),
            pltpu.VMEM((width, hid), BF),
            pltpu.VMEM((hid, width), BF),
            pltpu.VMEM((nz, ntok, pw), BF),
            pltpu.VMEM((GROUPS, count, slots), BF),
            pltpu.VMEM((GROUPS, nx, slots_x, sw), BF),
            pltpu.VMEM((GROUPS, 2, nx, slots_x, sw), BF),
            pltpu.VMEM((8, 2, 8, width), BF),
            pltpu.VMEM((GROUPS, 3, rows, hid), F32),
            pltpu.VMEM((GROUPS, 3, ny, quarter, hid), BF),
            pltpu.VMEM((GROUPS, rows, 128), F32),
            pltpu.VMEM((GROUPS, ny, quarter, 128), BF),
            pltpu.VMEM((GROUPS, 3, ny, quarter, hid), BF),
            pltpu.VMEM((GROUPS, ny, quarter, 128), BF),
            pltpu.VMEM((GROUPS, ny, quarter, 2 * hid), BF),
            pltpu.VMEM((GROUPS, ny, quarter, 128), BF),
            pltpu.VMEM((GROUPS, rows, 128), F32),
            pltpu.VMEM((GROUPS, rows, 128), F32),
            pltpu.VMEM((GROUPS, 2, nx, slots_x, width), BF),
            pltpu.VMEM((GROUPS, nx, slots_x, width), BF),
            pltpu.VMEM((GROUPS, nx, slots_x, width), BF),
            pltpu.VMEM((GROUPS, nx, slots_x, width), BF),
            pltpu.VMEM((nz, ntok, width), BF),
            pltpu.VMEM((nz, ntok, width), BF),
            dma((3,)),
            dma((2,)),
            dma((2 * far,)),
            dma((2 * far,)),
            dma((GROUPS, nx - 1)),
            dma((GROUPS, nx - 1)),
            dma((GROUPS, nx)),
            dma((GROUPS, nx)),
            dma((GROUPS, 4, ny - 1)),
            dma((GROUPS, 4, ny - 1)),
            dma((GROUPS, 2, ny - 1)),
            dma((GROUPS, 2, ny - 1)),
            dma((GROUPS, 2)),
            dma((GROUPS, nx)),
            dma((GROUPS, nx)),
            dma((GROUPS, nx - 1)),
            dma((GROUPS, nx - 1)),
            dma((nz - 1,)),
            dma((nz - 1,)),
        ],
        compiler_params=pltpu.CompilerParams(collective_id=0, has_side_effects=True),
        name="layer_backward",
    )(
        tokens,
        output_gradient,
        routes,
        router_expert_weight,
        tenant.reshape(ntok, 1),
        a_own,
        b_map,
        gate_weight[0],
        up_weight[0],
        down_weight[0],
    )
    adapter_a_grad = jnp.transpose(ag.reshape(2, 4, 8, width), (3, 0, 1, 2))[None]
    adapter_b_grad = bg.reshape(1, 2, 4, 16, hid)
    return (ig, adapter_a_grad, adapter_b_grad)


def solution(mesh):
    placed = (
        P("expert", "dp"),
        P("expert", "dp"),
        P("expert", None),
        P("expert", None),
        P("expert"),
        P("expert", "dp", None),
        P("expert", "dp", None),
        P("expert", None, "dp"),
        P("expert", "dp", None, None, None),
        P("expert", None, None, None, None),
    )
    return jax.shard_map(
        shards,
        mesh=mesh,
        in_specs=placed,
        out_specs=(
            P("expert", "dp"),
            P("expert", "dp", None, None, None),
            P("expert", None, None, None, None),
        ),
        check_vma=False,
    )
```

time: 91.5 us -> 83.7 us (0.915)
  Pallas kernels: 85.5 us -> 77.7 us
    pallas_call x1, Pallas kernels: 85.5 us -> 77.7 us  [shards(): pl.pallas_call(functools.partial(kernel, nx, nz, ny), out_shape=(jax.Shap...]
where the time goes in v3:
time: 83.7 us; the launch traced here: 83.4 us
  Pallas kernels  77.7 us (93%)
  local copies, waits for them, and re-layouts  5.06 us (6%)
    pallas_call x1, Pallas kernels, shards(): pl.pallas_call(functools.partial(kernel, nx, nz, ny), out_shape=(jax.Shap...  77.7 us
    unnamed x7, local copies, waits for them, and re-layouts  4.39 us

profile of v3, /device:TPU:1, one launch (start us, length us, event | category | flops | bytes accessed | tf_op | source)
XLA Modules:
  0.0 83.4 jit_solution(13958310539571205475)
XLA Ops:
  0.6 0.0 copy-start.1
  0.6 0.6 copy-done.1
  1.3 0.7 copy.13.ten
  2.0 77.7 %layer_backward.1 = (bf16[8,1024]{1,0:T(8,128)(2,1)}, f32[8,8,1024]{2,1,0:T(8,128)}, f32[128,512]{1,0:T(8,128)}) custom-call(bf16[8,1024]{1,0:T(8,128)(2,1)} %tok.1, bf16[8,1024]{1,0:T(8,128)(2,1)} %dy.1, s32[8,8]{1,0:T(8,128)} %routes.1, bf16[8,8]{1,0:T(8,128)(2,1)} %prob.1, s32[8,1]{1,0:T(8,128)} %copy.13.ten, bf16[8,8,1024]{2,1,0:T(8,128)(2,1)} %bitcast.21, ...), custom_call_target="tpu_custom_call" | custom-call | tf_op jit(solution)/shard_map/layer_backward/pallas_call | solution.py:474
  79.7 1.3 %copy.17 = bf16[8,1024]{1,0:T(8,128)(2,1)} copy(bf16[8,1024]{1,0:T(8,128)(2,1)} %get-tuple-element.12) | data formatting | bytes 32768
  81.0 0.0 copy-start
  81.0 1.7 %copy.18 = f32[1,1024,2,4,8]{1,4,3,2,0:T(8,128)} copy(f32[1,1024,2,4,8]{1,4,3,2,0:T(8,128)} %bitcast.20) | data formatting | bytes 524288
  82.7 0.0 copy-done
  82.7 0.7 copy.19
Async XLA Ops:
  0.6 0.7 copy-start.1
  81.0 1.7 %copy-start = (f32[128,512]{1,0:T(8,128)S(1)}, f32[128,512]{1,0:T(8,128)}, u32[]{:S(2)}) copy-start(f32[128,512]{1,0:T(8,128)} %get-tuple-element.8) | copy-start | bytes 786436

commit v4 on v3

--- a/solution.py
+++ b/solution.py
@@ -10,7 +10,7 @@
 ADAPTER_SCALE = 2.0
 CHIPS_X = 4
 HOP = 2
-GROUPS = 2
+GROUPS = 4
 BF = jnp.bfloat16
 F32 = jnp.float32
 MESH = pl.DeviceIdType.MESH
@@ -102,7 +102,10 @@
     sw = 2 * width + 128
     far = nz // 2
     gz = nz // GROUPS
-    off = gz // 2 - 1
+    spots = [0]
+    for d in range(1, far):
+        spots += [d, nz - d]
+    spots.append(far)
     slots_x = 2 * gz
     slots = nx * slots_x
     rows = 2 * slots
@@ -172,10 +175,10 @@
     weight = jnp.where(before == col_pos, weight, 0.0)
     lane_ten = lax.rem(lax.div(iota((ntok, 128), 1), 16), 4)
     ten_hot = (ten[...] == lane_ten).astype(F32)
-    pg[off, :, 0:width] = tok[...]
-    pg[off, :, width : 2 * width] = dy[...]
-    pg[off, :, 2 * width : 2 * width + lm] = weight.astype(BF)
-    pg[off, :, 2 * width + lm : pw] = ten_hot.astype(BF)
+    pg[0, :, 0:width] = tok[...]
+    pg[0, :, width : 2 * width] = dy[...]
+    pg[0, :, 2 * width : 2 * width + lm] = weight.astype(BF)
+    pg[0, :, 2 * width + lm : pw] = ten_hot.astype(BF)
     afull[:, c] = a_own[...]
 
     pl.semaphore_wait(barrier, len(near) + len(y_others))
@@ -186,7 +189,7 @@
     arrived = set()
 
     def place(direction, d):
-        return (off - d) % nz if direction == 0 else (off + d) % nz
+        return spots.index((nz - d) % nz if direction == 0 else d)
 
     def ring(direction, d):
         skip = min(d, HOP)
@@ -372,48 +375,49 @@
             rcopy(block, block, bx_s.at[g, i], bx_r.at[g, i], eid(o, z, c)).wait_recv()
         by_token = mm(sel[g], xb[g].reshape(slots, width))
         tz[g * gz : (g + 1) * gz] = by_token.reshape(gz, ntok, width).astype(BF)
-        dist = [(q - off) % nz for q in range(g * gz, (g + 1) * gz)]
+        dist = spots[g * gz : (g + 1) * gz]
         for d in sorted(dist, key=lambda d: -min(d, nz - d)):
-            q = (d + off) % nz
+            q = spots.index(d)
             if d == 0:
                 fb[0] = tz[q]
                 continue
             o = lax.rem(z + d, nz)
             send(rcopy(tz.at[q], fb.at[d], bz_s.at[d - 1], bz_r.at[d - 1], eid(x, o, c)))
 
-    step = min(HOP, far)
-    advance(1, step)
+    jumps = [(d, min(d + HOP - 1, far)) for d in range(1, far + 1, HOP)]
+
+    def start(g):
+        while jumps and len(jumps) > most_left(g):
+            advance(*jumps.pop(0))
+        for d in spots[g * gz : (g + 1) * gz]:
+            if d >= far:
+                need(0, nz - d)
+            else:
+                need(1, d)
+        select(g)
+        x_send(g)
+
+    def most_left(g):
+        return max(0, total_jumps - 1 - (g + 1) * total_jumps // GROUPS)
+
+    def products(g):
+        if g == 0:
+            rcopy(a_own, afull.at[:, 1 - c], a_sem.at[0], a_sem.at[1], partner).wait_recv()
+        c_recv(g)
+        partial(g)
+
+    def backward(g):
+        g_recv(g)
+        back_send(g)
+
+    total_jumps = len(jumps)
+    advance(*jumps.pop(0))
     send(a_copy)
-    advance(step + 1, max(step, far - HOP))
-    for d in range(1, off + 1):
-        need(0, d)
-    for d in range(1, gz - off):
-        need(1, d)
-    select(0)
-    x_send(0)
-    advance(max(step, far - HOP) + 1, far)
-    x_recv(0)
-    for d in range(1, far + 1):
-        need(0, d)
-        if d < far:
-            need(1, d)
-    select(1)
-    x_send(1)
-    rcopy(a_own, afull.at[:, 1 - c], a_sem.at[0], a_sem.at[1], partner).wait_recv()
-    c_recv(0)
-    partial(0)
-    x_recv(1)
-    act_grads(0)
-    c_recv(1)
-    partial(1)
-    g_recv(0)
-    back_send(0)
-    act_grads(1)
-    back_x(0)
-    home(0)
-    g_recv(1)
-    back_send(1)
-    back_x(1)
+    stages = [start, x_recv, products, act_grads, backward, back_x, home]
+    for tick in range(GROUPS + len(stages) - 2):
+        groups = [g for g in range(GROUPS) if 0 <= tick - g < len(stages)]
+        for g in groups if tick < GROUPS else groups[::-1]:
+            stages[tick - g](g)
 
     every = GROUPS * rows
     dg = dgu[:, :, :, 0:hid].reshape(every, hid)
@@ -421,7 +425,7 @@
     low_t = xsf[...].reshape(every, 128).astype(F32).T.astype(BF)
     bg_rows = iota((128, hid), 0)
     bg_out[...] = ADAPTER_SCALE * jnp.where(bg_rows < 64, mm(low_t, dg), mm(low_t, du))
-    home(1)
+    home(GROUPS - 1)
 
     for g in range(GROUPS):
         q_copy(g).wait_recv()

time: 83.7 us -> 78.2 us (0.934)
  the two profiles are of different devices: /device:TPU:1 before, /device:TPU:24 now
where the time goes in v4:
time: 78.2 us; the launch traced here: 78 us
  Pallas kernels  72.2 us (92%)
  local copies, waits for them, and re-layouts  5.06 us (6%)
    pallas_call x1, Pallas kernels, shards(): pl.pallas_call(functools.partial(kernel, nx, nz, ny), out_shape=(jax.Shap...  72.2 us
    unnamed x7, local copies, waits for them, and re-layouts  4.39 us

profile of v4, /device:TPU:24, one launch (start us, length us, event | category | flops | bytes accessed | tf_op | source)
XLA Modules:
  0.0 78.0 jit_solution(13267334533418828589)
XLA Ops:
  0.6 0.0 copy-start.1
  0.6 0.6 copy-done.1
  1.3 0.7 copy.13.ten
  2.0 72.2 %layer_backward.1 = (bf16[8,1024]{1,0:T(8,128)(2,1)}, f32[8,8,1024]{2,1,0:T(8,128)}, f32[128,512]{1,0:T(8,128)}) custom-call(bf16[8,1024]{1,0:T(8,128)(2,1)} %tok.1, bf16[8,1024]{1,0:T(8,128)(2,1)} %dy.1, s32[8,8]{1,0:T(8,128)} %routes.1, bf16[8,8]{1,0:T(8,128)(2,1)} %prob.1, s32[8,1]{1,0:T(8,128)} %copy.13.ten, bf16[8,8,1024]{2,1,0:T(8,128)(2,1)} %bitcast.21, ...), custom_call_target="tpu_custom_call" | custom-call | tf_op jit(solution)/shard_map/layer_backward/pallas_call | solution.py:478
  74.2 1.3 %copy.17 = bf16[8,1024]{1,0:T(8,128)(2,1)} copy(bf16[8,1024]{1,0:T(8,128)(2,1)} %get-tuple-element.12) | data formatting | bytes 32768
  75.5 0.0 copy-start
  75.5 1.7 %copy.18 = f32[1,1024,2,4,8]{1,4,3,2,0:T(8,128)} copy(f32[1,1024,2,4,8]{1,4,3,2,0:T(8,128)} %bitcast.20) | data formatting | bytes 524288
  77.3 0.0 copy-done
  77.3 0.7 copy.19
Async XLA Ops:
  0.6 0.7 copy-start.1
  75.5 1.7 %copy-start = (f32[128,512]{1,0:T(8,128)S(1)}, f32[128,512]{1,0:T(8,128)}, u32[]{:S(2)}) copy-start(f32[128,512]{1,0:T(8,128)} %get-tuple-element.8) | copy-start | bytes 786436
